TPU v7x, 128 devices: a whole 4x4x4 slice. The times are simulated.
128 devices in a mesh: samp: 8 (over z, core), pix: 16 (over x, y).
Axes of the slice: x: 4, y: 4, z: 4, core: 2. Of those that a mesh axis runs over, the one named last changes fastest.
Arguments:
- stamps: bfloat16 [8192, 16384], P(('samp', 'pix')), may hold values from -6 to 6
- start_panel: float32 [16384, 32], P('pix'), may hold values from -0.046875 to 0.046875
Outputs:
- eigen_psfs: float32 [16384, 32], P('pix')
All inputs are finite; a program needn't handle non-finite values.
Results may differ from a plain program's by a relative error of at most 0.025.
Values may be sent and summed in bfloat16 or wider, within the bound.
A program may use at most 64 MiB of HBM per device.

v0:
```python
import math

import jax
import jax.numpy as jnp
from jax import lax
from jax.sharding import PartitionSpec as P

PIX = 16384
ITERS = 10


def orthonormal(back, gram):
    lower = jnp.linalg.cholesky(gram)
    return lax.linalg.triangular_solve(lower, back, left_side=False, lower=True, transpose_a=True)


def gram_local(back):
    return jnp.dot(back.T, back, precision=lax.Precision.HIGHEST)


def local(stamps, start_panel):
    block = lax.all_to_all(stamps, "pix", split_axis=1, concat_axis=0, tiled=True)

    def sweep(step, panel):
        partial_value = jnp.dot(
            block, panel.astype(jnp.bfloat16), preferred_element_type=jnp.float32
        )
        proj = lax.psum(partial_value.astype(jnp.bfloat16), "pix")
        back = lax.dot_general(
            block, proj, (((0,), (0,)), ((), ())), preferred_element_type=jnp.float32
        )
        summed = lax.psum(back.astype(jnp.bfloat16), "samp").astype(jnp.float32)
        gram = lax.psum(gram_local(summed), "pix")
        return orthonormal(summed, gram)

    panel = lax.fori_loop(0, ITERS, sweep, start_panel)
    return panel * math.sqrt(PIX)


def solution(mesh):
    return jax.shard_map(
        local,
        mesh=mesh,
        in_specs=(P(("samp", "pix"), None), P("pix", None)),
        out_specs=P("pix", None),
        check_vma=False,
    )
```

profile of v0, /device:TPU:1, one launch (start us, length us, event | category | flops | bytes accessed | tf_op | source)
XLA Modules:
  0.0 2300.8 jit_solution(7996359796909041868)
XLA Ops:
  6.5 3.2 copy.9
  9.7 7.7 all-to-all-start
  17.4 27.9 %all-to-all-done = bf16[64,16,1024]{2,0,1:T(8,128)(2,1)S(1)} async-done(((bf16[64,16,1024]{2,0,1:T(8,128)(2,1)}), bf16[64,16,1024]{2,0,1:T(8,128)(2,1)S(1)}, u32[]{:S(2)}, u32[]{:S(2)}) %all-to-all-start) | async-done | bytes 2097184 | tf_op jit(solution)/shard_map/all_to_all | solution.py:22
  45.3 2247.9 %while.10 = (s32[]{:T(128)}, f32[1024,32]{0,1:T(8,128)S(1)}, bf16[1024,1024]{1,0:T(8,128)(2,1)S(1)}, s32[]{:T(128)}) while((s32[]{:T(128)}, f32[1024,32]{0,1:T(8,128)S(1)}, bf16[1024,1024]{1,0:T(8,128)(2,1)S(1)}, s32[]{:T(128)}) %tuple.26), condition=%wide.region_6.7_spmd, body=%wide.region_0.6_spmd.sunk | while | flops 149071904 | bytes 6013319 | solution.py:36
  46.8 87.0 %all-reduce.3.cloned.1.call-done = bf16[1024,32]{1,0:T(8,128)(2,1)} async-done(((bf16[1024,32]{1,0:T(8,128)(2,1)}), bf16[1024,32]{1,0:T(8,128)(2,1)}) %all-reduce.3.cloned.1.call-update) | async-done | bytes 65552 | tf_op jit(solution)/shard_map/while/body/eval_jaxpr/psum | solution.py:28
  133.8 2.1 fusion.34
  135.9 57.9 %all-reduce.5.cloned.1.call-done = bf16[1024,32]{0,1:T(8,128)(2,1)} async-done(((bf16[1024,32]{0,1:T(8,128)(2,1)}), bf16[1024,32]{0,1:T(8,128)(2,1)}) %all-reduce.5.cloned.1.call-update) | async-done | bytes 65552 | tf_op jit(solution)/shard_map/while/body/eval_jaxpr/psum | solution.py:32
  194.9 60.3 %psum.26 = f32[32,32]{0,1:T(8,128)S(1)} all-reduce(f32[32,32]{0,1:T(8,128)S(1)} %fusion.35), channel_id=1, replica_groups=mesh['samp'=8,'pix'=16] {'pix'}, use_global_device_ids=true, to_apply=%region_3.0 | all-reduce | flops 1024 | bytes 8192 | tf_op jit(solution)/shard_map/while/body/eval_jaxpr/psum | solution.py:33
  255.2 2.9 cholesky.58
  259.5 2.4 custom-call.7
  264.6 95.1 %all-reduce.3.cloned.1.call-done = bf16[1024,32]{1,0:T(8,128)(2,1)} async-done(((bf16[1024,32]{1,0:T(8,128)(2,1)}), bf16[1024,32]{1,0:T(8,128)(2,1)}) %all-reduce.3.cloned.1.call-update) | async-done | bytes 65552 | tf_op jit(solution)/shard_map/while/body/eval_jaxpr/psum | solution.py:28
  359.6 2.1 fusion.34
  361.7 57.7 %all-reduce.5.cloned.1.call-done = bf16[1024,32]{0,1:T(8,128)(2,1)} async-done(((bf16[1024,32]{0,1:T(8,128)(2,1)}), bf16[1024,32]{0,1:T(8,128)(2,1)}) %all-reduce.5.cloned.1.call-update) | async-done | bytes 65552 | tf_op jit(solution)/shard_map/while/body/eval_jaxpr/psum | solution.py:32
  420.5 60.3 %psum.26 = f32[32,32]{0,1:T(8,128)S(1)} all-reduce(f32[32,32]{0,1:T(8,128)S(1)} %fusion.35), channel_id=1, replica_groups=mesh['samp'=8,'pix'=16] {'pix'}, use_global_device_ids=true, to_apply=%region_3.0 | all-reduce | flops 1024 | bytes 8192 | tf_op jit(solution)/shard_map/while/body/eval_jaxpr/psum | solution.py:33
  480.9 2.9 cholesky.58
  485.2 2.4 custom-call.7
  490.2 94.8 %all-reduce.3.cloned.1.call-done = bf16[1024,32]{1,0:T(8,128)(2,1)} async-done(((bf16[1024,32]{1,0:T(8,128)(2,1)}), bf16[1024,32]{1,0:T(8,128)(2,1)}) %all-reduce.3.cloned.1.call-update) | async-done | bytes 65552 | tf_op jit(solution)/shard_map/while/body/eval_jaxpr/psum | solution.py:28
  585.0 2.1 fusion.34
  587.1 57.7 %all-reduce.5.cloned.1.call-done = bf16[1024,32]{0,1:T(8,128)(2,1)} async-done(((bf16[1024,32]{0,1:T(8,128)(2,1)}), bf16[1024,32]{0,1:T(8,128)(2,1)}) %all-reduce.5.cloned.1.call-update) | async-done | bytes 65552 | tf_op jit(solution)/shard_map/while/body/eval_jaxpr/psum | solution.py:32
  645.9 60.3 %psum.26 = f32[32,32]{0,1:T(8,128)S(1)} all-reduce(f32[32,32]{0,1:T(8,128)S(1)} %fusion.35), channel_id=1, replica_groups=mesh['samp'=8,'pix'=16] {'pix'}, use_global_device_ids=true, to_apply=%region_3.0 | all-reduce | flops 1024 | bytes 8192 | tf_op jit(solution)/shard_map/while/body/eval_jaxpr/psum | solution.py:33
  706.3 2.9 cholesky.58
  710.5 2.4 custom-call.7
  715.6 95.1 %all-reduce.3.cloned.1.call-done = bf16[1024,32]{1,0:T(8,128)(2,1)} async-done(((bf16[1024,32]{1,0:T(8,128)(2,1)}), bf16[1024,32]{1,0:T(8,128)(2,1)}) %all-reduce.3.cloned.1.call-update) | async-done | bytes 65552 | tf_op jit(solution)/shard_map/while/body/eval_jaxpr/psum | solution.py:28
  810.7 2.1 fusion.34
  812.8 57.9 %all-reduce.5.cloned.1.call-done = bf16[1024,32]{0,1:T(8,128)(2,1)} async-done(((bf16[1024,32]{0,1:T(8,128)(2,1)}), bf16[1024,32]{0,1:T(8,128)(2,1)}) %all-reduce.5.cloned.1.call-update) | async-done | bytes 65552 | tf_op jit(solution)/shard_map/while/body/eval_jaxpr/psum | solution.py:32
  871.7 60.3 %psum.26 = f32[32,32]{0,1:T(8,128)S(1)} all-reduce(f32[32,32]{0,1:T(8,128)S(1)} %fusion.35), channel_id=1, replica_groups=mesh['samp'=8,'pix'=16] {'pix'}, use_global_device_ids=true, to_apply=%region_3.0 | all-reduce | flops 1024 | bytes 8192 | tf_op jit(solution)/shard_map/while/body/eval_jaxpr/psum | solution.py:33
  932.1 2.9 cholesky.58
  936.3 2.4 custom-call.7
  941.4 95.1 %all-reduce.3.cloned.1.call-done = bf16[1024,32]{1,0:T(8,128)(2,1)} async-done(((bf16[1024,32]{1,0:T(8,128)(2,1)}), bf16[1024,32]{1,0:T(8,128)(2,1)}) %all-reduce.3.cloned.1.call-update) | async-done | bytes 65552 | tf_op jit(solution)/shard_map/while/body/eval_jaxpr/psum | solution.py:28
  1036.5 2.1 fusion.34
  1038.6 57.7 %all-reduce.5.cloned.1.call-done = bf16[1024,32]{0,1:T(8,128)(2,1)} async-done(((bf16[1024,32]{0,1:T(8,128)(2,1)}), bf16[1024,32]{0,1:T(8,128)(2,1)}) %all-reduce.5.cloned.1.call-update) | async-done | bytes 65552 | tf_op jit(solution)/shard_map/while/body/eval_jaxpr/psum | solution.py:32
  1097.3 60.3 %psum.26 = f32[32,32]{0,1:T(8,128)S(1)} all-reduce(f32[32,32]{0,1:T(8,128)S(1)} %fusion.35), channel_id=1, replica_groups=mesh['samp'=8,'pix'=16] {'pix'}, use_global_device_ids=true, to_apply=%region_3.0 | all-reduce | flops 1024 | bytes 8192 | tf_op jit(solution)/shard_map/while/body/eval_jaxpr/psum | solution.py:33
  1157.7 2.9 cholesky.58
  1162.0 2.4 custom-call.7
  1167.1 95.1 %all-reduce.3.cloned.1.call-done = bf16[1024,32]{1,0:T(8,128)(2,1)} async-done(((bf16[1024,32]{1,0:T(8,128)(2,1)}), bf16[1024,32]{1,0:T(8,128)(2,1)}) %all-reduce.3.cloned.1.call-update) | async-done | bytes 65552 | tf_op jit(solution)/shard_map/while/body/eval_jaxpr/psum | solution.py:28
  1262.1 2.1 fusion.34
  1264.2 57.7 %all-reduce.5.cloned.1.call-done = bf16[1024,32]{0,1:T(8,128)(2,1)} async-done(((bf16[1024,32]{0,1:T(8,128)(2,1)}), bf16[1024,32]{0,1:T(8,128)(2,1)}) %all-reduce.5.cloned.1.call-update) | async-done | bytes 65552 | tf_op jit(solution)/shard_map/while/body/eval_jaxpr/psum | solution.py:32
  1323.0 60.3 %psum.26 = f32[32,32]{0,1:T(8,128)S(1)} all-reduce(f32[32,32]{0,1:T(8,128)S(1)} %fusion.35), channel_id=1, replica_groups=mesh['samp'=8,'pix'=16] {'pix'}, use_global_device_ids=true, to_apply=%region_3.0 | all-reduce | flops 1024 | bytes 8192 | tf_op jit(solution)/shard_map/while/body/eval_jaxpr/psum | solution.py:33
  1383.4 2.9 cholesky.58
  1387.7 2.4 custom-call.7
  1392.7 95.1 %all-reduce.3.cloned.1.call-done = bf16[1024,32]{1,0:T(8,128)(2,1)} async-done(((bf16[1024,32]{1,0:T(8,128)(2,1)}), bf16[1024,32]{1,0:T(8,128)(2,1)}) %all-reduce.3.cloned.1.call-update) | async-done | bytes 65552 | tf_op jit(solution)/shard_map/while/body/eval_jaxpr/psum | solution.py:28
  1487.8 2.1 fusion.34
  1489.9 57.7 %all-reduce.5.cloned.1.call-done = bf16[1024,32]{0,1:T(8,128)(2,1)} async-done(((bf16[1024,32]{0,1:T(8,128)(2,1)}), bf16[1024,32]{0,1:T(8,128)(2,1)}) %all-reduce.5.cloned.1.call-update) | async-done | bytes 65552 | tf_op jit(solution)/shard_map/while/body/eval_jaxpr/psum | solution.py:32
  1548.7 60.3 %psum.26 = f32[32,32]{0,1:T(8,128)S(1)} all-reduce(f32[32,32]{0,1:T(8,128)S(1)} %fusion.35), channel_id=1, replica_groups=mesh['samp'=8,'pix'=16] {'pix'}, use_global_device_ids=true, to_apply=%region_3.0 | all-reduce | flops 1024 | bytes 8192 | tf_op jit(solution)/shard_map/while/body/eval_jaxpr/psum | solution.py:33
  1609.1 2.9 cholesky.58
  1613.3 2.4 custom-call.7
  1618.4 94.8 %all-reduce.3.cloned.1.call-done = bf16[1024,32]{1,0:T(8,128)(2,1)} async-done(((bf16[1024,32]{1,0:T(8,128)(2,1)}), bf16[1024,32]{1,0:T(8,128)(2,1)}) %all-reduce.3.cloned.1.call-update) | async-done | bytes 65552 | tf_op jit(solution)/shard_map/while/body/eval_jaxpr/psum | solution.py:28
  1713.2 2.1 fusion.34
  1715.3 57.7 %all-reduce.5.cloned.1.call-done = bf16[1024,32]{0,1:T(8,128)(2,1)} async-done(((bf16[1024,32]{0,1:T(8,128)(2,1)}), bf16[1024,32]{0,1:T(8,128)(2,1)}) %all-reduce.5.cloned.1.call-update) | async-done | bytes 65552 | tf_op jit(solution)/shard_map/while/body/eval_jaxpr/psum | solution.py:32
  1774.1 60.3 %psum.26 = f32[32,32]{0,1:T(8,128)S(1)} all-reduce(f32[32,32]{0,1:T(8,128)S(1)} %fusion.35), channel_id=1, replica_groups=mesh['samp'=8,'pix'=16] {'pix'}, use_global_device_ids=true, to_apply=%region_3.0 | all-reduce | flops 1024 | bytes 8192 | tf_op jit(solution)/shard_map/while/body/eval_jaxpr/psum | solution.py:33
  1834.4 2.9 cholesky.58
  1838.7 2.4 custom-call.7
  1843.8 94.8 %all-reduce.3.cloned.1.call-done = bf16[1024,32]{1,0:T(8,128)(2,1)} async-done(((bf16[1024,32]{1,0:T(8,128)(2,1)}), bf16[1024,32]{1,0:T(8,128)(2,1)}) %all-reduce.3.cloned.1.call-update) | async-done | bytes 65552 | tf_op jit(solution)/shard_map/while/body/eval_jaxpr/psum | solution.py:28
  1938.5 2.1 fusion.34
  1940.6 57.7 %all-reduce.5.cloned.1.call-done = bf16[1024,32]{0,1:T(8,128)(2,1)} async-done(((bf16[1024,32]{0,1:T(8,128)(2,1)}), bf16[1024,32]{0,1:T(8,128)(2,1)}) %all-reduce.5.cloned.1.call-update) | async-done | bytes 65552 | tf_op jit(solution)/shard_map/while/body/eval_jaxpr/psum | solution.py:32
  1999.4 60.3 %psum.26 = f32[32,32]{0,1:T(8,128)S(1)} all-reduce(f32[32,32]{0,1:T(8,128)S(1)} %fusion.35), channel_id=1, replica_groups=mesh['samp'=8,'pix'=16] {'pix'}, use_global_device_ids=true, to_apply=%region_3.0 | all-reduce | flops 1024 | bytes 8192 | tf_op jit(solution)/shard_map/while/body/eval_jaxpr/psum | solution.py:33
  2059.8 2.9 cholesky.58
  2064.0 2.4 custom-call.7
  2069.1 95.1 %all-reduce.3.cloned.1.call-done = bf16[1024,32]{1,0:T(8,128)(2,1)} async-done(((bf16[1024,32]{1,0:T(8,128)(2,1)}), bf16[1024,32]{1,0:T(8,128)(2,1)}) %all-reduce.3.cloned.1.call-update) | async-done | bytes 65552 | tf_op jit(solution)/shard_map/while/body/eval_jaxpr/psum | solution.py:28
  2164.2 2.1 fusion.34
  2166.3 57.7 %all-reduce.5.cloned.1.call-done = bf16[1024,32]{0,1:T(8,128)(2,1)} async-done(((bf16[1024,32]{0,1:T(8,128)(2,1)}), bf16[1024,32]{0,1:T(8,128)(2,1)}) %all-reduce.5.cloned.1.call-update) | async-done | bytes 65552 | tf_op jit(solution)/shard_map/while/body/eval_jaxpr/psum | solution.py:32
  2225.1 60.3 %psum.26 = f32[32,32]{0,1:T(8,128)S(1)} all-reduce(f32[32,32]{0,1:T(8,128)S(1)} %fusion.35), channel_id=1, replica_groups=mesh['samp'=8,'pix'=16] {'pix'}, use_global_device_ids=true, to_apply=%region_3.0 | all-reduce | flops 1024 | bytes 8192 | tf_op jit(solution)/shard_map/while/body/eval_jaxpr/psum | solution.py:33
  2285.5 2.9 cholesky.58
  2289.7 2.4 custom-call.7
  (123 shorter events, 51.3 us)
Async XLA Ops:
  9.7 35.6 %copy-start = (f32[1024,32]{0,1:T(8,128)S(1)}, f32[1024,32]{0,1:T(8,128)}, u32[]{:S(2)}) copy-start(f32[1024,32]{0,1:T(8,128)} %param.5) | copy-start | bytes 393220
  9.7 35.6 %all-to-all-start = ((bf16[64,16,1024]{2,0,1:T(8,128)(2,1)}), bf16[64,16,1024]{2,0,1:T(8,128)(2,1)S(1)}, u32[]{:S(2)}, u32[]{:S(2)}) async-start(bf16[64,16,1024]{2,0,1:T(8,128)(2,1)} %bitcast.45), calls=%async_computation | async-start | bytes 4194304 | tf_op jit(solution)/shard_map/all_to_all | solution.py:22
  45.3 88.5 %all-reduce.3.cloned.1.call-start = ((), (), s32[]{:S(2)}) async-start(), calls=%async_computation.1 | async-start | bytes 524288 | tf_op jit(solution)/shard_map/while/body/eval_jaxpr/psum | solution.py:28
  46.7 147.1 %all-reduce.5.cloned.1.call-start = ((), (), s32[]{:S(2)}) async-start(), calls=%async_computation.2 | async-start | bytes 131072 | tf_op jit(solution)/shard_map/while/body/eval_jaxpr/psum | solution.py:32
  263.1 96.6 %all-reduce.3.cloned.1.call-start = ((), (), s32[]{:S(2)}) async-start(), calls=%async_computation.1 | async-start | bytes 524288 | tf_op jit(solution)/shard_map/while/body/eval_jaxpr/psum | solution.py:28
  264.5 155.0 %all-reduce.5.cloned.1.call-start = ((), (), s32[]{:S(2)}) async-start(), calls=%async_computation.2 | async-start | bytes 131072 | tf_op jit(solution)/shard_map/while/body/eval_jaxpr/psum | solution.py:32
  488.7 96.3 %all-reduce.3.cloned.1.call-start = ((), (), s32[]{:S(2)}) async-start(), calls=%async_computation.1 | async-start | bytes 524288 | tf_op jit(solution)/shard_map/while/body/eval_jaxpr/psum | solution.py:28
  490.2 154.6 %all-reduce.5.cloned.1.call-start = ((), (), s32[]{:S(2)}) async-start(), calls=%async_computation.2 | async-start | bytes 131072 | tf_op jit(solution)/shard_map/while/body/eval_jaxpr/psum | solution.py:32
  714.1 96.6 %all-reduce.3.cloned.1.call-start = ((), (), s32[]{:S(2)}) async-start(), calls=%async_computation.1 | async-start | bytes 524288 | tf_op jit(solution)/shard_map/while/body/eval_jaxpr/psum | solution.py:28
  715.5 155.1 %all-reduce.5.cloned.1.call-start = ((), (), s32[]{:S(2)}) async-start(), calls=%async_computation.2 | async-start | bytes 131072 | tf_op jit(solution)/shard_map/while/body/eval_jaxpr/psum | solution.py:32
  939.9 96.6 %all-reduce.3.cloned.1.call-start = ((), (), s32[]{:S(2)}) async-start(), calls=%async_computation.1 | async-start | bytes 524288 | tf_op jit(solution)/shard_map/while/body/eval_jaxpr/psum | solution.py:28
  941.4 154.9 %all-reduce.5.cloned.1.call-start = ((), (), s32[]{:S(2)}) async-start(), calls=%async_computation.2 | async-start | bytes 131072 | tf_op jit(solution)/shard_map/while/body/eval_jaxpr/psum | solution.py:32
  1165.6 96.6 %all-reduce.3.cloned.1.call-start = ((), (), s32[]{:S(2)}) async-start(), calls=%async_computation.1 | async-start | bytes 524288 | tf_op jit(solution)/shard_map/while/body/eval_jaxpr/psum | solution.py:28
  1167.0 155.0 %all-reduce.5.cloned.1.call-start = ((), (), s32[]{:S(2)}) async-start(), calls=%async_computation.2 | async-start | bytes 131072 | tf_op jit(solution)/shard_map/while/body/eval_jaxpr/psum | solution.py:32
  1391.2 96.6 %all-reduce.3.cloned.1.call-start = ((), (), s32[]{:S(2)}) async-start(), calls=%async_computation.1 | async-start | bytes 524288 | tf_op jit(solution)/shard_map/while/body/eval_jaxpr/psum | solution.py:28
  1392.7 155.0 %all-reduce.5.cloned.1.call-start = ((), (), s32[]{:S(2)}) async-start(), calls=%async_computation.2 | async-start | bytes 131072 | tf_op jit(solution)/shard_map/while/body/eval_jaxpr/psum | solution.py:32
  1616.9 96.3 %all-reduce.3.cloned.1.call-start = ((), (), s32[]{:S(2)}) async-start(), calls=%async_computation.1 | async-start | bytes 524288 | tf_op jit(solution)/shard_map/while/body/eval_jaxpr/psum | solution.py:28
  1618.4 154.6 %all-reduce.5.cloned.1.call-start = ((), (), s32[]{:S(2)}) async-start(), calls=%async_computation.2 | async-start | bytes 131072 | tf_op jit(solution)/shard_map/while/body/eval_jaxpr/psum | solution.py:32
  1842.3 96.3 %all-reduce.3.cloned.1.call-start = ((), (), s32[]{:S(2)}) async-start(), calls=%async_computation.1 | async-start | bytes 524288 | tf_op jit(solution)/shard_map/while/body/eval_jaxpr/psum | solution.py:28
  1843.7 154.7 %all-reduce.5.cloned.1.call-start = ((), (), s32[]{:S(2)}) async-start(), calls=%async_computation.2 | async-start | bytes 131072 | tf_op jit(solution)/shard_map/while/body/eval_jaxpr/psum | solution.py:32
  2067.6 96.6 %all-reduce.3.cloned.1.call-start = ((), (), s32[]{:S(2)}) async-start(), calls=%async_computation.1 | async-start | bytes 524288 | tf_op jit(solution)/shard_map/while/body/eval_jaxpr/psum | solution.py:28
  2069.1 155.0 %all-reduce.5.cloned.1.call-start = ((), (), s32[]{:S(2)}) async-start(), calls=%async_computation.2 | async-start | bytes 131072 | tf_op jit(solution)/shard_map/while/body/eval_jaxpr/psum | solution.py:32
Sparse Core Ops, SparseCore 0:
  49.3 84.4 all-reduce.2
  136.2 57.5 all-reduce.4
  267.1 92.5 all-reduce.2
  361.9 57.5 all-reduce.4
  492.4 92.5 all-reduce.2
  587.3 57.5 all-reduce.4
  718.1 92.5 all-reduce.2
  813.1 57.5 all-reduce.4
  943.9 92.5 all-reduce.2
  1038.7 57.5 all-reduce.4
  1169.6 92.5 all-reduce.2
  1264.4 57.5 all-reduce.4
  1395.2 92.5 all-reduce.2
  1490.1 57.5 all-reduce.4
  1620.6 92.5 all-reduce.2
  1715.4 57.5 all-reduce.4
  1846.0 92.5 all-reduce.2
  1940.8 57.5 all-reduce.4
  2071.6 92.5 all-reduce.2
  2166.5 57.5 all-reduce.4
where the time goes:
time: 2320 us; the launch traced here: 2300 us
  waiting for transfers between devices  1550 us (67%)
  blocking collectives  603 us (26%)
  other arithmetic  67.5 us (3%)
  matrix products  56.1 us (2%)
    psum x10, waiting for transfers between devices, sweep(): proj = lax.psum(partial_value.astype(jnp.bfloat16), 'pix')  942 us
    psum x10, blocking collectives, sweep(): gram = lax.psum(gram_local(summed), 'pix')  603 us
    psum x10, waiting for transfers between devices, sweep(): summed = lax.psum(back.astype(jnp.bfloat16), 'samp').astype(jnp.float32)  578 us
  transfers between devices with their start and end apart: 21, of which 21 were waited for; matrix products, arithmetic and copies ran while one was open for 0% of the time, Pallas kernels for 0%

commit v1 on v0

v1 whole, which is shorter than its diff:
```python
import functools

import jax
import jax.numpy as jnp
from jax import lax
from jax.experimental import pallas as pl
from jax.experimental.pallas import tpu as pltpu
from jax.sharding import PartitionSpec as P

PIX = 16384
K = 32
ITERS = 10
SCALE = 128.0
GX, GY = 4, 4
NP = GX * GY
NS = 8
ROWS = 64
SB = NP * ROWS
PB = PIX // NP
HK = K // 2
MESH = pl.DeviceIdType.MESH
NT = (((1,), (1,)), ((), ()))
BF, F32 = jnp.bfloat16, jnp.float32

PIX_STEPS = sorted(
    ((dx, dy) for dx in range(GX) for dy in range(GY) if dx or dy),
    key=lambda d: -(min(d[0], GX - d[0]) + min(d[1], GY - d[1])),
)
SAMP_STEPS = [4, 5, 3, 2, 6, 7, 1]


def split3(a):
    hi = a.astype(BF)
    rest = a - hi.astype(F32)
    mid = rest.astype(BF)
    return hi, mid, (rest - mid.astype(F32)).astype(BF)


def inverse_cholesky(gram):
    rows = lax.broadcasted_iota(jnp.int32, (K, K), 0)
    cols = lax.broadcasted_iota(jnp.int32, (K, K), 1)
    work = jnp.concatenate([gram, jnp.where(rows == cols, 1.0, 0.0).astype(F32)], axis=1)
    below = lax.broadcasted_iota(jnp.int32, (K, 1), 0)
    for j in range(K):
        pivot = lax.rsqrt(work[j : j + 1, j : j + 1])
        row = work[j : j + 1, :] * pivot
        column = work[:, j : j + 1] * pivot
        work = jnp.where(
            below > j, work - column * row, jnp.where(below == j, row, work)
        )
    return work[:, K:]


def pack_gram(gram):
    return jnp.concatenate([gram[8 * i : 8 * i + 8, :] for i in range(4)], axis=1)


def unpack_gram(packed):
    return jnp.concatenate([packed[:, K * i : K * i + K] for i in range(4)], axis=0)


def kernel(
    stamps, start, out,
    block, blockt, panel, part1, got1, proj, gram_out, gram_in, part2, got2,
    sems, gram_sems,
):
    s, p = lax.axis_index("samp"), lax.axis_index("pix")
    x, y = p // GY, p % GY

    def pix_peer(dx, dy):
        return ((x + dx) % GX) * GY + (y + dy) % GY

    def samp_peer(d):
        return (s + d) % NS

    def send(src, dst, sem, arrived=None, **device):
        pltpu.make_async_remote_copy(
            src_ref=src, dst_ref=dst, send_sem=sems.at[sem],
            recv_sem=sems.at[sem + 1] if arrived is None else arrived,
            device_id=device, device_id_type=MESH,
        ).start()

    def wait_on(ref, sem):
        pltpu.make_async_copy(ref, ref, sem).wait()

    def wait(ref, sem):
        wait_on(ref, sems.at[sem])

    barrier = pltpu.get_barrier_semaphore()
    for dx, dy in PIX_STEPS:
        pl.semaphore_signal(barrier, inc=1, device_id={"pix": pix_peer(dx, dy)}, device_id_type=MESH)
    for d in SAMP_STEPS:
        pl.semaphore_signal(barrier, inc=1, device_id={"samp": samp_peer(d)}, device_id_type=MESH)
    pl.semaphore_wait(barrier, NP - 1 + NS - 1)

    mine = block.at[pl.ds(pl.multiple_of(p * ROWS, ROWS), ROWS)]

    def pixels_of(q):
        return stamps.at[:, pl.ds(pl.multiple_of(q * PB, PB), PB)]

    for dx, dy in PIX_STEPS:
        q = pix_peer(dx, dy)
        send(pixels_of(q), mine, 0, pix=q)
    own = pltpu.make_async_copy(pixels_of(p), mine, sems.at[14])
    own.start()

    first = start[...].T.astype(BF)
    for i in range(NS):
        panel[i] = first[:, 128 * i : 128 * i + 128]

    own.wait()
    wait(block.at[pl.ds(0, SB - ROWS)], 1)
    wait(block.at[pl.ds(0, SB - ROWS)], 0)
    blockt[...] = block[...].T

    def whole_panel():
        return jnp.concatenate([panel[i] for i in range(NS)], axis=1)

    def share_gram(slot, partial):
        gram_out[...] = pack_gram(partial)
        for i, (dx, dy) in enumerate(PIX_STEPS):
            send(gram_out, gram_in.at[slot, i], 4, gram_sems.at[slot], pix=pix_peer(dx, dy))

    def sum_gram(slot):
        wait_on(gram_in.at[slot], gram_sems.at[slot])
        total = gram_out[...]
        for i in range(NP - 1):
            total = total + gram_in[slot, i]
        wait(gram_in.at[slot], 4)
        return unpack_gram(total)

    def gram_of(now):
        return lax.dot_general(now, now, NT, preferred_element_type=F32)

    def sweep(step, carry):
        now = whole_panel()
        partial = jnp.dot(now, blockt[...], preferred_element_type=F32).astype(BF)
        for q in range(NP):
            c, h = q // 2, q % 2
            part1[q] = partial[HK * h : HK * h + HK, 128 * c : 128 * c + 128]
        for i, (dx, dy) in enumerate(PIX_STEPS):
            q = pix_peer(dx, dy)
            send(part1.at[q], got1.at[i], 2, pix=q)
        rows = lax.broadcasted_iota(jnp.int32, (K, K), 0)
        cols = lax.broadcasted_iota(jnp.int32, (K, K), 1)
        unit = jnp.where(rows == cols, 1.0 / NP, 0.0).astype(F32)
        slot = lax.rem(step, 2)
        share_gram(slot, jnp.where(step == 0, unit, gram_of(now)))

        wait(got1, 3)
        total = part1[p].astype(F32)
        for i in range(NP - 1):
            total = total + got1[i].astype(F32)
        proj[p] = total.astype(BF)
        for dx, dy in PIX_STEPS:
            send(proj.at[p], proj.at[p], 6, pix=pix_peer(dx, dy))
        wait(got1, 2)

        hi, mid, low = split3(inverse_cholesky(sum_gram(slot)))
        left = jnp.concatenate([hi, mid, low], axis=1)

        wait(proj.at[pl.ds(0, NP - 1)], 7)
        wait(proj.at[pl.ds(0, NP - 1)], 6)
        raw = jnp.concatenate(
            [jnp.concatenate([proj[2 * c], proj[2 * c + 1]], axis=0) for c in range(NP // 2)], axis=1
        )
        scaled = jnp.dot(
            left, jnp.concatenate([raw, raw, raw], axis=0), preferred_element_type=F32
        ).astype(BF)
        back = jnp.dot(scaled, block[...], preferred_element_type=F32).astype(BF)
        for r in range(NS):
            part2[r] = back[:, 128 * r : 128 * r + 128]
        for i, d in enumerate(SAMP_STEPS):
            r = samp_peer(d)
            send(part2.at[r], got2.at[i], 8, samp=r)
        wait(got2, 9)
        total = part2[s].astype(F32)
        for i in range(NS - 1):
            total = total + got2[i].astype(F32)
        panel[s] = total.astype(BF)
        for d in SAMP_STEPS:
            send(panel.at[s], panel.at[s], 10, samp=samp_peer(d))
        wait(got2, 8)
        wait(panel.at[pl.ds(0, NS - 1)], 11)
        wait(panel.at[pl.ds(0, NS - 1)], 10)
        return carry

    lax.fori_loop(0, ITERS, sweep, 0)

    now = whole_panel()
    share_gram(ITERS % 2, gram_of(now))
    hi, mid, low = split3(inverse_cholesky(sum_gram(ITERS % 2)) * SCALE)
    left = jnp.concatenate([hi, mid, low], axis=1)
    out[...] = jnp.dot(left, jnp.concatenate([now, now, now], axis=0), preferred_element_type=F32)


def local(stamps, start_panel):
    vmem = pl.BlockSpec(memory_space=pltpu.VMEM)
    result = pl.pallas_call(
        kernel,
        out_shape=jax.ShapeDtypeStruct((K, PB), F32),
        in_specs=[pl.BlockSpec(memory_space=pl.ANY), vmem],
        out_specs=vmem,
        scratch_shapes=[
            pltpu.VMEM((SB, PB), BF),
            pltpu.VMEM((PB, SB), BF),
            pltpu.VMEM((NS, K, 128), BF),
            pltpu.VMEM((NP, HK, 128), BF),
            pltpu.VMEM((NP - 1, HK, 128), BF),
            pltpu.VMEM((NP, HK, 128), BF),
            pltpu.VMEM((8, 128), F32),
            pltpu.VMEM((2, NP - 1, 8, 128), F32),
            pltpu.VMEM((NS, K, 128), BF),
            pltpu.VMEM((NS - 1, K, 128), BF),
            pltpu.SemaphoreType.DMA((15,)),
            pltpu.SemaphoreType.DMA((2,)),
        ],
        compiler_params=pltpu.CompilerParams(
            collective_id=0, has_side_effects=True, vmem_limit_bytes=48 << 20
        ),
    )(stamps, start_panel)
    return result.T


def solution(mesh):
    return jax.shard_map(
        local,
        mesh=mesh,
        in_specs=(P(("samp", "pix"), None), P("pix", None)),
        out_specs=P("pix", None),
        check_vma=False,
    )
```

time: 2320 us -> 220 us (0.09)
  waiting for transfers between devices: 1550 us -> 0 us
  blocking collectives: 603 us -> 0 us
  Pallas kernels: 0 us -> 217 us
  other arithmetic: 67.5 us -> 0 us
  matrix products: 56.1 us -> 0 us
    psum x20 -> x0, waiting for transfers between devices: 1520 us -> none  [the longest x10 942 us: sweep(): proj = lax.psum(partial_value.astype(jnp.bfloat16), 'pix')]
    psum x10 -> x0, blocking collectives: 603 us -> none  [sweep(): gram = lax.psum(gram_local(summed), 'pix')]
    pallas_call x0 -> x1, Pallas kernels: none -> 217 us  [local(): pl.pallas_call(kernel, out_shape=jax.ShapeDtypeStruct((K, PB), F32), in_s...]
    another operation x50 -> x0, other arithmetic: 66.8 us -> none  [the longest x30 35.9 us: orthonormal(): lower = jnp.linalg.cholesky(gram)]
    dot_general x30 -> x0, matrix products: 45 us -> none  [the longest x10 20.7 us: sweep(): lax.dot_general(block, proj, (((0,), (0,)), ((), ())), preferred_element_...]
    all_to_all x1 -> x0, waiting for transfers between devices: 27.9 us -> none  [local(): lax.all_to_all(stamps, 'pix', split_axis=1, concat_axis=0, tiled=True)]
  transfers between devices with their start and end apart: 21 -> 0, of which waited for: 21 -> 0; matrix products, arithmetic and copies ran while one was open for 0% -> 0% of each run, Pallas kernels for 0% -> 0%
where the time goes in v1:
time: 220 us
  Pallas kernels  217 us (99%)
  local copies, waits for them, and re-layouts  3.34 us (2%)
    pallas_call x1, Pallas kernels, local(): pl.pallas_call(kernel, out_shape=jax.ShapeDtypeStruct((K, PB), F32), in_s...  217 us

profile of v1, /device:TPU:1, one launch (start us, length us, event | category | flops | bytes accessed | tf_op | source)
XLA Modules:
  0.0 220.3 jit_solution(6495206755576794012)
XLA Ops:
  0.0 1.1 copy.3.start
  1.1 0.0 copy-start
  1.1 1.6 copy-done
  2.7 216.9 %shard_map.28 = f32[32,1024]{1,0:T(8,128)S(1)} custom-call(bf16[64,16384]{1,0:T(8,128)(2,1)S(1)} %copy-done, f32[1024,32]{1,0:T(8,128)S(1)} %copy.3.start), custom_call_target="tpu_custom_call" | custom-call | tf_op jit(solution)/shard_map/pallas_call | solution.py:199
  219.6 0.7 copy.5
Async XLA Ops:
  1.1 1.6 copy-start

commit v2 on v0

v2 whole, which is shorter than its diff:
```python
import jax
import jax.numpy as jnp
from jax import lax
from jax.experimental import pallas as pl
from jax.experimental.pallas import tpu as pltpu
from jax.sharding import PartitionSpec as P

PIX = 16384
K = 32
ITERS = 10
SCALE = 128.0
GX, GY, GZ = 4, 4, 4
CHIPS = GX * GY
ROWS = 64
SB = CHIPS * 2 * ROWS
PC = PIX // CHIPS
PB = PC // 2
HK = K // 2
LANES = 128
TILES = PB // LANES
MESH = pl.DeviceIdType.MESH
NT = (((1,), (1,)), ((), ()))
BF, F32 = jnp.bfloat16, jnp.float32


def hops(offset):
    return sum(min(d, 4 - d) for d in offset)


OFFSETS = sorted(((dx, dy) for dx in range(GX) for dy in range(GY)), key=hops)
BACK = [OFFSETS.index(((-dx) % GX, (-dy) % GY)) for dx, dy in OFFSETS]
FAR_FIRST = list(range(CHIPS - 1, 0, -1))
Z_STEPS = [2, 1, 3]


def split3(a):
    hi = a.astype(BF)
    rest = a - hi.astype(F32)
    mid = rest.astype(BF)
    return hi, mid, (rest - mid.astype(F32)).astype(BF)


def inverse_cholesky(gram):
    rows = lax.broadcasted_iota(jnp.int32, (K, K), 0)
    cols = lax.broadcasted_iota(jnp.int32, (K, K), 1)
    work = jnp.concatenate([gram, jnp.where(rows == cols, 1.0, 0.0).astype(F32)], axis=1)
    below = lax.broadcasted_iota(jnp.int32, (K, 1), 0)
    for j in range(K):
        pivot = lax.rsqrt(work[j : j + 1, j : j + 1])
        row = work[j : j + 1, :] * pivot
        column = work[:, j : j + 1] * pivot
        work = jnp.where(
            below > j, work - column * row, jnp.where(below == j, row, work)
        )
    return work[:, K:]


def apply_factor(factor, value):
    f, v = split3(factor), split3(value)
    pairs = [(0, 0), (0, 1), (1, 0), (1, 1), (0, 2), (2, 0)]
    left = jnp.concatenate([f[i] for i, _ in pairs], axis=1)
    right = jnp.concatenate([v[j] for _, j in pairs], axis=0)
    return jnp.dot(left, right, preferred_element_type=F32)


def pack_gram(gram):
    return jnp.concatenate([gram[8 * i : 8 * i + 8, :] for i in range(4)], axis=1)


def unpack_gram(packed):
    return jnp.concatenate([packed[:, K * i : K * i + K] for i in range(4)], axis=0)


def kernel(
    stamps, start, out,
    block, blockt, panel, part1, got1, proj, gram_out, gram_core, gram_chip, gram_in, sums, pair,
    sems, core_sems, gram_sems, z_sems,
):
    s, p = lax.axis_index("samp"), lax.axis_index("pix")
    x, y, z, c = p // GY, p % GY, s // 2, s % 2

    def device(slot, core):
        dx, dy = OFFSETS[slot]
        return {"samp": z * 2 + core, "pix": ((x + dx) % GX) * GY + (y + dy) % GY}

    def at_z(dz):
        return {"samp": ((z + dz) % GZ) * 2 + c, "pix": p}

    other = 1 - c

    def send(src, dst, sem, to, arrived=None):
        pltpu.make_async_remote_copy(
            src_ref=src, dst_ref=dst, send_sem=sems.at[sem],
            recv_sem=sems.at[sem + 1] if arrived is None else arrived,
            device_id=to, device_id_type=MESH,
        ).start()

    def wait_on(ref, sem):
        pltpu.make_async_copy(ref, ref, sem).wait()

    def wait(ref, sem):
        wait_on(ref, sems.at[sem])

    barrier = pltpu.get_barrier_semaphore()
    for slot in FAR_FIRST:
        for core in range(2):
            pl.semaphore_signal(barrier, inc=1, device_id=device(slot, core), device_id_type=MESH)
    for dz in Z_STEPS:
        pl.semaphore_signal(barrier, inc=1, device_id=at_z(dz), device_id_type=MESH)
    pl.semaphore_signal(barrier, inc=1, device_id=device(0, other), device_id_type=MESH)
    pl.semaphore_wait(barrier, 2 * CHIPS - 1 + GZ - 1)

    def rows_of(slot):
        return block.at[pl.ds(pl.multiple_of(slot * 2 * ROWS + c * ROWS, ROWS), ROWS)]

    def pixels_of(to, core):
        return stamps.at[:, pl.ds(pl.multiple_of(to["pix"] * PC + core * PB, PB), PB)]

    for slot in FAR_FIRST:
        for core in range(2):
            to = device(slot, core)
            send(pixels_of(to, core), rows_of(BACK[slot]), 0, to)
    to = device(0, other)
    send(pixels_of(to, other), rows_of(0), 0, to)
    own = pltpu.make_async_copy(pixels_of(device(0, c), c), rows_of(0), sems.at[14])
    own.start()

    panel[...] = start[:, pl.ds(pl.multiple_of(c * PB, PB), PB)].astype(BF)

    own.wait()
    wait(block.at[pl.ds(0, SB - ROWS)], 1)
    wait(block.at[pl.ds(0, SB - ROWS)], 0)
    blockt[...] = block[...].T

    def share_gram(turn, partial):
        gram_out[...] = pack_gram(partial)
        send(gram_out, gram_core.at[turn], 4, device(0, other), core_sems.at[turn])

    def share_chip_gram(turn):
        wait_on(gram_core.at[turn], core_sems.at[turn])
        gram_chip[...] = gram_out[...] + gram_core[turn]
        wait(gram_out, 4)
        for slot in FAR_FIRST:
            send(gram_chip, gram_in.at[turn, BACK[slot] - 1], 6, device(slot, c), gram_sems.at[turn])

    def sum_gram(turn):
        wait_on(gram_in.at[turn], gram_sems.at[turn])
        total = gram_chip[...]
        for i in range(CHIPS - 1):
            total = total + gram_in[turn, i]
        wait(gram_in.at[turn], 6)
        return unpack_gram(total)

    def gram_of(now):
        return lax.dot_general(now, now, NT, preferred_element_type=F32)

    def sweep(step, carry):
        turn = lax.rem(step, 2)
        now = panel[...]
        for group in (1, 0):
            first = group * CHIPS // 2
            lanes = pl.ds(first * LANES, CHIPS // 2 * LANES)
            partial = jnp.dot(now, blockt[:, lanes], preferred_element_type=F32).astype(BF)
            for i in range(CHIPS // 2):
                for core in range(2):
                    part1[first + i, core] = partial[HK * core : HK * core + HK, LANES * i : LANES * i + LANES]
            for slot in range(first + CHIPS // 2 - 1, first - 1, -1):
                if slot:
                    for core in range(2):
                        send(part1.at[slot, core], got1.at[BACK[slot] * 2 - 1 + c], 2, device(slot, core))
        send(part1.at[0, other], got1.at[0], 2, device(0, other))
        rows = lax.broadcasted_iota(jnp.int32, (K, K), 0)
        cols = lax.broadcasted_iota(jnp.int32, (K, K), 1)
        unit = jnp.where(rows == cols, 1.0 / (2 * CHIPS), 0.0).astype(F32)
        share_gram(turn, jnp.where(step == 0, unit, gram_of(now)))

        wait(got1, 3)
        total = part1[0, c].astype(F32)
        for i in range(2 * CHIPS - 1):
            total = total + got1[i].astype(F32)
        proj[0, c] = total.astype(BF)
        for slot in FAR_FIRST:
            for core in range(2):
                send(proj.at[0, c], proj.at[BACK[slot], c], 8, device(slot, core))
        send(proj.at[0, c], proj.at[0, c], 8, device(0, other))
        wait(got1, 2)
        share_chip_gram(turn)

        wait(got1, 9)
        wait(got1, 8)
        raw = jnp.concatenate(
            [jnp.concatenate([proj[i, 0], proj[i, 1]], axis=0) for i in range(CHIPS)], axis=1
        )
        back = jnp.dot(raw, block[...], preferred_element_type=F32).astype(BF)
        sums[turn, z] = back
        for dz in Z_STEPS:
            send(sums.at[turn, z], sums.at[turn, z], 10, at_z(dz), z_sems.at[turn])

        factor = inverse_cholesky(sum_gram(turn))
        wait_on(sums.at[turn, pl.ds(0, GZ - 1)], z_sems.at[turn])
        wait(sums.at[turn, pl.ds(0, GZ - 1)], 10)
        total = sums[turn, 0].astype(F32)
        for i in range(1, GZ):
            total = total + sums[turn, i].astype(F32)
        panel[...] = apply_factor(factor, total).astype(BF)
        return carry

    lax.fori_loop(0, ITERS, sweep, 0)

    now = panel[...]
    send(panel, pair, 12, device(0, other))
    share_gram(ITERS % 2, gram_of(now))
    share_chip_gram(ITERS % 2)
    wait(pair, 13)
    wait(pair, 12)
    factor = inverse_cholesky(sum_gram(ITERS % 2)) * SCALE
    out[:, pl.ds(pl.multiple_of(c * PB, PB), PB)] = apply_factor(factor, now.astype(F32))
    out[:, pl.ds(pl.multiple_of(other * PB, PB), PB)] = apply_factor(factor, pair[...].astype(F32))


def local(stamps, start_panel):
    vmem = pl.BlockSpec(memory_space=pltpu.VMEM)
    result = pl.pallas_call(
        kernel,
        out_shape=jax.ShapeDtypeStruct((K, PC), F32),
        in_specs=[pl.BlockSpec(memory_space=pltpu.HBM), vmem],
        out_specs=vmem,
        scratch_shapes=[
            pltpu.VMEM((SB, PB), BF),
            pltpu.VMEM((PB, SB), BF),
            pltpu.VMEM((K, PB), BF),
            pltpu.VMEM((CHIPS, 2, HK, LANES), BF),
            pltpu.VMEM((2 * CHIPS - 1, HK, LANES), BF),
            pltpu.VMEM((CHIPS, 2, HK, LANES), BF),
            pltpu.VMEM((8, LANES), F32),
            pltpu.VMEM((2, 8, LANES), F32),
            pltpu.VMEM((8, LANES), F32),
            pltpu.VMEM((2, CHIPS - 1, 8, LANES), F32),
            pltpu.VMEM((2, GZ, K, PB), BF),
            pltpu.VMEM((K, PB), BF),
            pltpu.SemaphoreType.DMA((15,)),
            pltpu.SemaphoreType.DMA((2,)),
            pltpu.SemaphoreType.DMA((2,)),
            pltpu.SemaphoreType.DMA((2,)),
        ],
        compiler_params=pltpu.CompilerParams(
            collective_id=0, has_side_effects=True, vmem_limit_bytes=63 << 20
        ),
    )(stamps, start_panel.T)
    return result.T


def solution(mesh):
    return jax.shard_map(
        local,
        mesh=mesh,
        in_specs=(P(("samp", "pix"), None), P("pix", None)),
        out_specs=P("pix", None),
        check_vma=False,
    )
```

time: 2320 us -> 197 us (0.08)
  waiting for transfers between devices: 1550 us -> 0 us
  blocking collectives: 603 us -> 0 us
  Pallas kernels: 0 us -> 195 us
  other arithmetic: 67.5 us -> 0 us
  matrix products: 56.1 us -> 0 us
    psum x20 -> x0, waiting for transfers between devices: 1520 us -> none  [the longest x10 942 us: sweep(): proj = lax.psum(partial_value.astype(jnp.bfloat16), 'pix')]
    psum x10 -> x0, blocking collectives: 603 us -> none  [sweep(): gram = lax.psum(gram_local(summed), 'pix')]
    pallas_call x0 -> x1, Pallas kernels: none -> 195 us  [local(): pl.pallas_call(kernel, out_shape=jax.ShapeDtypeStruct((K, PC), F32), in_s...]
    another operation x50 -> x0, other arithmetic: 66.8 us -> none  [the longest x30 35.9 us: orthonormal(): lower = jnp.linalg.cholesky(gram)]
    dot_general x30 -> x0, matrix products: 45 us -> none  [the longest x10 20.7 us: sweep(): lax.dot_general(block, proj, (((0,), (0,)), ((), ())), preferred_element_...]
    all_to_all x1 -> x0, waiting for transfers between devices: 27.9 us -> none  [local(): lax.all_to_all(stamps, 'pix', split_axis=1, concat_axis=0, tiled=True)]
  transfers between devices with their start and end apart: 21 -> 0, of which waited for: 21 -> 0; matrix products, arithmetic and copies ran while one was open for 0% -> 0% of each run, Pallas kernels for 0% -> 0%
where the time goes in v2:
time: 197 us; the launch traced here: 196 us
  Pallas kernels  195 us (99%)
    pallas_call x1, Pallas kernels, local(): pl.pallas_call(kernel, out_shape=jax.ShapeDtypeStruct((K, PC), F32), in_s...  195 us

profile of v2, /device:TPU:1, one launch (start us, length us, event | category | flops | bytes accessed | tf_op | source)
XLA Modules:
  0.0 196.5 jit_solution(15462915397924624831)
XLA Ops:
  0.0 194.9 %shard_map.28 = f32[32,1024]{1,0:T(8,128)} custom-call(bf16[64,16384]{1,0:T(8,128)(2,1)} %stamps.1, f32[32,1024]{1,0:T(8,128)} %bitcast.3), custom_call_target="tpu_custom_call" | custom-call | tf_op jit(solution)/shard_map/pallas_call | solution.py:223
  194.9 1.6 copy.4

commit v3 on v2

--- a/solution.py
+++ b/solution.py
@@ -30,6 +30,8 @@
 OFFSETS = sorted(((dx, dy) for dx in range(GX) for dy in range(GY)), key=hops)
 BACK = [OFFSETS.index(((-dx) % GX, (-dy) % GY)) for dx, dy in OFFSETS]
 FAR_FIRST = list(range(CHIPS - 1, 0, -1))
+GROUPS = [(0, 4), (4, 10), (10, 14), (14, 16)]
+GROUP_OF = [g for g, (first, last) in enumerate(GROUPS) for _ in range(first, last)]
 Z_STEPS = [2, 1, 3]
 
 
@@ -45,12 +47,18 @@
     cols = lax.broadcasted_iota(jnp.int32, (K, K), 1)
     work = jnp.concatenate([gram, jnp.where(rows == cols, 1.0, 0.0).astype(F32)], axis=1)
     below = lax.broadcasted_iota(jnp.int32, (K, 1), 0)
-    for j in range(K):
-        pivot = lax.rsqrt(work[j : j + 1, j : j + 1])
-        row = work[j : j + 1, :] * pivot
+    for j in range(0, K, 2):
+        one, two = work[j : j + 1, :], work[j + 1 : j + 2, :]
+        pivot = lax.rsqrt(one[:, j : j + 1])
+        under = two[:, j : j + 1] * pivot
+        pivot2 = lax.rsqrt(two[:, j + 1 : j + 2] - under * under)
+        row = one * pivot
+        row2 = (two - under * row) * pivot2
         column = work[:, j : j + 1] * pivot
+        column2 = (work[:, j + 1 : j + 2] - under * column) * pivot2
+        rest = work - column * row - column2 * row2
         work = jnp.where(
-            below > j, work - column * row, jnp.where(below == j, row, work)
+            below > j + 1, rest, jnp.where(below == j, row, jnp.where(below == j + 1, row2, work))
         )
     return work[:, K:]
 
@@ -73,8 +81,8 @@
 
 def kernel(
     stamps, start, out,
-    block, blockt, panel, part1, got1, proj, gram_out, gram_core, gram_chip, gram_in, sums, pair,
-    sems, core_sems, gram_sems, z_sems,
+    block, blockt, initial, panel, part1, got1, proj, gram_out, gram_core, gram_chip, gram_in, gram_all, sums, pair,
+    sems, group_sems, core_sems, gram_sems, z_sems,
 ):
     s, p = lax.axis_index("samp"), lax.axis_index("pix")
     x, y, z, c = p // GY, p % GY, s // 2, s % 2
@@ -116,21 +124,20 @@
     def pixels_of(to, core):
         return stamps.at[:, pl.ds(pl.multiple_of(to["pix"] * PC + core * PB, PB), PB)]
 
+    def arrival(slot):
+        return group_sems.at[GROUP_OF[slot]]
+
     for slot in FAR_FIRST:
         for core in range(2):
             to = device(slot, core)
-            send(pixels_of(to, core), rows_of(BACK[slot]), 0, to)
+            send(pixels_of(to, core), rows_of(BACK[slot]), 0, to, arrival(BACK[slot]))
     to = device(0, other)
-    send(pixels_of(to, other), rows_of(0), 0, to)
+    send(pixels_of(to, other), rows_of(0), 0, to, arrival(0))
     own = pltpu.make_async_copy(pixels_of(device(0, c), c), rows_of(0), sems.at[14])
     own.start()
 
-    panel[...] = start[:, pl.ds(pl.multiple_of(c * PB, PB), PB)].astype(BF)
-
-    own.wait()
-    wait(block.at[pl.ds(0, SB - ROWS)], 1)
-    wait(block.at[pl.ds(0, SB - ROWS)], 0)
-    blockt[...] = block[...].T
+    begin = pltpu.make_async_copy(start.at[:, pl.ds(pl.multiple_of(c * PB, PB), PB)], initial, sems.at[15])
+    begin.start()
 
     def share_gram(turn, partial):
         gram_out[...] = pack_gram(partial)
@@ -154,26 +161,22 @@
     def gram_of(now):
         return lax.dot_general(now, now, NT, preferred_element_type=F32)
 
-    def sweep(step, carry):
-        turn = lax.rem(step, 2)
-        now = panel[...]
-        for group in (1, 0):
-            first = group * CHIPS // 2
-            lanes = pl.ds(first * LANES, CHIPS // 2 * LANES)
-            partial = jnp.dot(now, blockt[:, lanes], preferred_element_type=F32).astype(BF)
-            for i in range(CHIPS // 2):
+    def add_up_stamps(now, group):
+        first, last = GROUPS[group]
+        partial = jnp.dot(
+            now, blockt[:, first * LANES : last * LANES], preferred_element_type=F32
+        ).astype(BF)
+        for i in range(last - first):
+            for core in range(2):
+                part1[first + i, core] = partial[HK * core : HK * core + HK, LANES * i : LANES * i + LANES]
+        for slot in range(last - 1, first - 1, -1):
+            if slot:
                 for core in range(2):
-                    part1[first + i, core] = partial[HK * core : HK * core + HK, LANES * i : LANES * i + LANES]
-            for slot in range(first + CHIPS // 2 - 1, first - 1, -1):
-                if slot:
-                    for core in range(2):
-                        send(part1.at[slot, core], got1.at[BACK[slot] * 2 - 1 + c], 2, device(slot, core))
-        send(part1.at[0, other], got1.at[0], 2, device(0, other))
-        rows = lax.broadcasted_iota(jnp.int32, (K, K), 0)
-        cols = lax.broadcasted_iota(jnp.int32, (K, K), 1)
-        unit = jnp.where(rows == cols, 1.0 / (2 * CHIPS), 0.0).astype(F32)
-        share_gram(turn, jnp.where(step == 0, unit, gram_of(now)))
-
+                    send(part1.at[slot, core], got1.at[BACK[slot] * 2 - 1 + c], 2, device(slot, core))
+            else:
+                send(part1.at[0, other], got1.at[0], 2, device(0, other))
+
+    def spread_stamps():
         wait(got1, 3)
         total = part1[0, c].astype(F32)
         for i in range(2 * CHIPS - 1):
@@ -181,39 +184,78 @@
         proj[0, c] = total.astype(BF)
         for slot in FAR_FIRST:
             for core in range(2):
-                send(proj.at[0, c], proj.at[BACK[slot], c], 8, device(slot, core))
-        send(proj.at[0, c], proj.at[0, c], 8, device(0, other))
+                send(proj.at[0, c], proj.at[BACK[slot], c], 8, device(slot, core), arrival(BACK[slot]))
+        send(proj.at[0, c], proj.at[0, c], 8, device(0, other), arrival(0))
         wait(got1, 2)
-        share_chip_gram(turn)
-
-        wait(got1, 9)
-        wait(got1, 8)
-        raw = jnp.concatenate(
-            [jnp.concatenate([proj[i, 0], proj[i, 1]], axis=0) for i in range(CHIPS)], axis=1
-        )
-        back = jnp.dot(raw, block[...], preferred_element_type=F32).astype(BF)
-        sums[turn, z] = back
+
+    def add_up_pixels(turn):
+        back = jnp.zeros((K, PB), F32)
+        for group, (first, last) in enumerate(GROUPS):
+            pieces = 2 * (last - first) - (first == 0)
+            wait_on(got1.at[pl.ds(0, pieces)], arrival(first))
+            raw = jnp.concatenate(
+                [jnp.concatenate([proj[i, 0], proj[i, 1]], axis=0) for i in range(first, last)], axis=1
+            )
+            back = back + jnp.dot(
+                raw, block[first * LANES : last * LANES, :], preferred_element_type=F32
+            )
+        sums[turn, z] = back.astype(BF)
         for dz in Z_STEPS:
             send(sums.at[turn, z], sums.at[turn, z], 10, at_z(dz), z_sems.at[turn])
-
-        factor = inverse_cholesky(sum_gram(turn))
+        wait(got1, 8)
+
+    def sum_pixels(turn):
         wait_on(sums.at[turn, pl.ds(0, GZ - 1)], z_sems.at[turn])
         wait(sums.at[turn, pl.ds(0, GZ - 1)], 10)
         total = sums[turn, 0].astype(F32)
         for i in range(1, GZ):
             total = total + sums[turn, i].astype(F32)
-        panel[...] = apply_factor(factor, total).astype(BF)
+        return total
+
+    begin.wait()
+    own.wait()
+    now = initial[...].astype(BF)
+    for group in reversed(range(len(GROUPS))):
+        first, last = GROUPS[group]
+        remote = (last - first) * 2 * ROWS - (ROWS if first == 0 else 0)
+        wait_on(block.at[pl.ds(0, remote)], arrival(first))
+        blockt[:, first * LANES : last * LANES] = block[first * LANES : last * LANES, :].T
+        add_up_stamps(now, group)
+    wait(block.at[pl.ds(0, SB - ROWS)], 0)
+    spread_stamps()
+    add_up_pixels(0)
+    panel[...] = sum_pixels(0).astype(BF)
+
+    def sweep(step, carry):
+        turn = lax.rem(step, 2)
+        now = panel[...]
+        for group in reversed(range(len(GROUPS))):
+            add_up_stamps(now, group)
+        share_gram(turn, gram_of(now))
+        spread_stamps()
+        share_chip_gram(turn)
+        add_up_pixels(turn)
+        factor = inverse_cholesky(sum_gram(turn))
+        panel[...] = apply_factor(factor, sum_pixels(turn)).astype(BF)
         return carry
 
-    lax.fori_loop(0, ITERS, sweep, 0)
+    lax.fori_loop(1, ITERS, sweep, 0)
 
     now = panel[...]
     send(panel, pair, 12, device(0, other))
-    share_gram(ITERS % 2, gram_of(now))
-    share_chip_gram(ITERS % 2)
+    gram_all[0, c] = pack_gram(gram_of(now))
+    for slot in FAR_FIRST:
+        for core in range(2):
+            send(gram_all.at[0, c], gram_all.at[BACK[slot], c], 6, device(slot, core))
+    send(gram_all.at[0, c], gram_all.at[0, c], 6, device(0, other))
     wait(pair, 13)
     wait(pair, 12)
-    factor = inverse_cholesky(sum_gram(ITERS % 2)) * SCALE
+    wait(got1, 7)
+    wait(got1, 6)
+    total = gram_all[0, 0] + gram_all[0, 1]
+    for slot in range(1, CHIPS):
+        total = total + (gram_all[slot, 0] + gram_all[slot, 1])
+    factor = inverse_cholesky(unpack_gram(total)) * SCALE
     out[:, pl.ds(pl.multiple_of(c * PB, PB), PB)] = apply_factor(factor, now.astype(F32))
     out[:, pl.ds(pl.multiple_of(other * PB, PB), PB)] = apply_factor(factor, pair[...].astype(F32))
 
@@ -223,11 +265,12 @@
     result = pl.pallas_call(
         kernel,
         out_shape=jax.ShapeDtypeStruct((K, PC), F32),
-        in_specs=[pl.BlockSpec(memory_space=pltpu.HBM), vmem],
+        in_specs=[pl.BlockSpec(memory_space=pl.ANY)] * 2,
         out_specs=vmem,
         scratch_shapes=[
             pltpu.VMEM((SB, PB), BF),
             pltpu.VMEM((PB, SB), BF),
+            pltpu.VMEM((K, PB), F32),
             pltpu.VMEM((K, PB), BF),
             pltpu.VMEM((CHIPS, 2, HK, LANES), BF),
             pltpu.VMEM((2 * CHIPS - 1, HK, LANES), BF),
@@ -236,9 +279,11 @@
             pltpu.VMEM((2, 8, LANES), F32),
             pltpu.VMEM((8, LANES), F32),
             pltpu.VMEM((2, CHIPS - 1, 8, LANES), F32),
+            pltpu.VMEM((CHIPS, 2, 8, LANES), F32),
             pltpu.VMEM((2, GZ, K, PB), BF),
             pltpu.VMEM((K, PB), BF),
-            pltpu.SemaphoreType.DMA((15,)),
+            pltpu.SemaphoreType.DMA((16,)),
+            pltpu.SemaphoreType.DMA((len(GROUPS),)),
             pltpu.SemaphoreType.DMA((2,)),
             pltpu.SemaphoreType.DMA((2,)),
             pltpu.SemaphoreType.DMA((2,)),

time: 197 us -> 194 us (0.985)
  Pallas kernels: 195 us -> 192 us
    pallas_call x1, Pallas kernels: 195 us -> 192 us  [local(): pl.pallas_call(kernel, out_shape=jax.ShapeDtypeStruct((K, PC), F32), in_s...]
where the time goes in v3:
time: 194 us
  Pallas kernels  192 us (99%)
    pallas_call x1, Pallas kernels, local(): pl.pallas_call(kernel, out_shape=jax.ShapeDtypeStruct((K, PC), F32), in_s...  192 us

profile of v3, /device:TPU:1, one launch (start us, length us, event | category | flops | bytes accessed | tf_op | source)
XLA Modules:
  0.0 193.7 jit_solution(4901029787542545840)
XLA Ops:
  0.0 192.1 %shard_map.28 = f32[32,1024]{1,0:T(8,128)} custom-call(bf16[64,16384]{1,0:T(8,128)(2,1)} %stamps.1, f32[32,1024]{1,0:T(8,128)} %bitcast.3), custom_call_target="tpu_custom_call" | custom-call | tf_op jit(solution)/shard_map/pallas_call | solution.py:265
  192.1 1.6 copy.4

commit v4 on v3

--- a/solution.py
+++ b/solution.py
@@ -27,10 +27,19 @@
     return sum(min(d, 4 - d) for d in offset)
 
 
-OFFSETS = sorted(((dx, dy) for dx in range(GX) for dy in range(GY)), key=hops)
+def opposite(offset):
+    return (offset[0] + GX // 2) % GX, (offset[1] + GY // 2) % GY
+
+
+ALL = sorted(((dx, dy) for dx in range(GX) for dy in range(GY)), key=hops)
+OFFSETS = []
+for near in ALL:
+    if near not in OFFSETS:
+        OFFSETS += [near, opposite(near)]
 BACK = [OFFSETS.index(((-dx) % GX, (-dy) % GY)) for dx, dy in OFFSETS]
-FAR_FIRST = list(range(CHIPS - 1, 0, -1))
-GROUPS = [(0, 4), (4, 10), (10, 14), (14, 16)]
+HOPS = [hops(offset) for offset in OFFSETS]
+FAR_FIRST = sorted(range(1, CHIPS), key=lambda slot: -HOPS[slot])
+GROUPS = [(0, 4), (4, 10), (10, 16)]
 GROUP_OF = [g for g, (first, last) in enumerate(GROUPS) for _ in range(first, last)]
 Z_STEPS = [2, 1, 3]
 
@@ -82,7 +91,7 @@
 def kernel(
     stamps, start, out,
     block, blockt, initial, panel, part1, got1, proj, gram_out, gram_core, gram_chip, gram_in, gram_all, sums, pair,
-    sems, group_sems, core_sems, gram_sems, z_sems,
+    sems, group_sems, got_sems, core_sems, gram_sems, z_sems,
 ):
     s, p = lax.axis_index("samp"), lax.axis_index("pix")
     x, y, z, c = p // GY, p % GY, s // 2, s % 2
@@ -127,7 +136,7 @@
     def arrival(slot):
         return group_sems.at[GROUP_OF[slot]]
 
-    for slot in FAR_FIRST:
+    for slot in sorted(range(1, CHIPS), key=lambda slot: GROUP_OF[slot]):
         for core in range(2):
             to = device(slot, core)
             send(pixels_of(to, core), rows_of(BACK[slot]), 0, to, arrival(BACK[slot]))
@@ -161,38 +170,54 @@
     def gram_of(now):
         return lax.dot_general(now, now, NT, preferred_element_type=F32)
 
-    def add_up_stamps(now, group):
+    def send_part(turn, slot, core):
+        place = BACK[slot] * 2 - 1 + c if slot else 0
+        send(part1.at[slot, core], got1.at[turn, place], 2, device(slot, core), got_sems.at[turn])
+
+    def add_up_stamps(now, turn, group):
         first, last = GROUPS[group]
         partial = jnp.dot(
             now, blockt[:, first * LANES : last * LANES], preferred_element_type=F32
         ).astype(BF)
-        for i in range(last - first):
+        for slot in range(first, last):
             for core in range(2):
-                part1[first + i, core] = partial[HK * core : HK * core + HK, LANES * i : LANES * i + LANES]
-        for slot in range(last - 1, first - 1, -1):
-            if slot:
+                piece = partial[HK * core : HK * core + HK, LANES * (slot - first) : LANES * (slot - first + 1)]
+                part1[slot, core, 0] = piece
+                part1[slot ^ 1, core, 1] = piece
+        for slot in FAR_FIRST:
+            if first <= slot < last and HOPS[slot] > 1:
                 for core in range(2):
-                    send(part1.at[slot, core], got1.at[BACK[slot] * 2 - 1 + c], 2, device(slot, core))
-            else:
-                send(part1.at[0, other], got1.at[0], 2, device(0, other))
-
-    def spread_stamps():
-        wait(got1, 3)
+                    send_part(turn, slot, core)
+
+    def spread_stamps(turn):
+        for slot in FAR_FIRST:
+            if HOPS[slot] == 1:
+                for core in range(2):
+                    send_part(turn, slot, core)
+        send_part(turn, 0, other)
+
+    def gather_stamps(turn):
+        wait_on(got1.at[turn], got_sems.at[turn])
         total = part1[0, c].astype(F32)
         for i in range(2 * CHIPS - 1):
-            total = total + got1[i].astype(F32)
-        proj[0, c] = total.astype(BF)
+            total = total + got1[turn, i].astype(F32)
+        proj[0, c] = total[0].astype(BF)
+        proj[1, c] = total[1].astype(BF)
+        both = proj.at[pl.ds(0, 2), c]
         for slot in FAR_FIRST:
             for core in range(2):
-                send(proj.at[0, c], proj.at[BACK[slot], c], 8, device(slot, core), arrival(BACK[slot]))
-        send(proj.at[0, c], proj.at[0, c], 8, device(0, other), arrival(0))
-        wait(got1, 2)
+                if HOPS[slot] == 2:
+                    send(proj.at[0, c], proj.at[BACK[slot], c], 8, device(slot, core), arrival(BACK[slot]))
+                elif HOPS[slot] == 1:
+                    send(both, proj.at[pl.ds(BACK[slot], 2), c], 8, device(slot, core), arrival(BACK[slot]))
+        send(both, both, 8, device(0, other), arrival(0))
+        wait(got1.at[turn], 2)
 
     def add_up_pixels(turn):
         back = jnp.zeros((K, PB), F32)
-        for group, (first, last) in enumerate(GROUPS):
-            pieces = 2 * (last - first) - (first == 0)
-            wait_on(got1.at[pl.ds(0, pieces)], arrival(first))
+        for first, last in GROUPS:
+            tiles = 2 * (last - first) - (2 if first == 0 else 0)
+            wait_on(got1.at[0, pl.ds(0, tiles // 2)], arrival(first))
             raw = jnp.concatenate(
                 [jnp.concatenate([proj[i, 0], proj[i, 1]], axis=0) for i in range(first, last)], axis=1
             )
@@ -202,7 +227,7 @@
         sums[turn, z] = back.astype(BF)
         for dz in Z_STEPS:
             send(sums.at[turn, z], sums.at[turn, z], 10, at_z(dz), z_sems.at[turn])
-        wait(got1, 8)
+        wait(proj.at[pl.ds(0, CHIPS - 1)], 8)
 
     def sum_pixels(turn):
         wait_on(sums.at[turn, pl.ds(0, GZ - 1)], z_sems.at[turn])
@@ -215,24 +240,26 @@
     begin.wait()
     own.wait()
     now = initial[...].astype(BF)
-    for group in reversed(range(len(GROUPS))):
+    for group in range(len(GROUPS)):
         first, last = GROUPS[group]
         remote = (last - first) * 2 * ROWS - (ROWS if first == 0 else 0)
         wait_on(block.at[pl.ds(0, remote)], arrival(first))
         blockt[:, first * LANES : last * LANES] = block[first * LANES : last * LANES, :].T
-        add_up_stamps(now, group)
+        add_up_stamps(now, 0, group)
+    spread_stamps(0)
     wait(block.at[pl.ds(0, SB - ROWS)], 0)
-    spread_stamps()
+    gather_stamps(0)
     add_up_pixels(0)
     panel[...] = sum_pixels(0).astype(BF)
 
     def sweep(step, carry):
         turn = lax.rem(step, 2)
         now = panel[...]
-        for group in reversed(range(len(GROUPS))):
-            add_up_stamps(now, group)
+        for group in range(len(GROUPS)):
+            add_up_stamps(now, turn, group)
+        spread_stamps(turn)
         share_gram(turn, gram_of(now))
-        spread_stamps()
+        gather_stamps(turn)
         share_chip_gram(turn)
         add_up_pixels(turn)
         factor = inverse_cholesky(sum_gram(turn))
@@ -250,8 +277,9 @@
     send(gram_all.at[0, c], gram_all.at[0, c], 6, device(0, other))
     wait(pair, 13)
     wait(pair, 12)
-    wait(got1, 7)
-    wait(got1, 6)
+    every = got1.at[0, :, 0]
+    wait(every, 7)
+    wait(every, 6)
     total = gram_all[0, 0] + gram_all[0, 1]
     for slot in range(1, CHIPS):
         total = total + (gram_all[slot, 0] + gram_all[slot, 1])
@@ -272,8 +300,8 @@
             pltpu.VMEM((PB, SB), BF),
             pltpu.VMEM((K, PB), F32),
             pltpu.VMEM((K, PB), BF),
-            pltpu.VMEM((CHIPS, 2, HK, LANES), BF),
-            pltpu.VMEM((2 * CHIPS - 1, HK, LANES), BF),
+            pltpu.VMEM((CHIPS, 2, 2, HK, LANES), BF),
+            pltpu.VMEM((2, 2 * CHIPS - 1, 2, HK, LANES), BF),
             pltpu.VMEM((CHIPS, 2, HK, LANES), BF),
             pltpu.VMEM((8, LANES), F32),
             pltpu.VMEM((2, 8, LANES), F32),
@@ -287,6 +315,7 @@
             pltpu.SemaphoreType.DMA((2,)),
             pltpu.SemaphoreType.DMA((2,)),
             pltpu.SemaphoreType.DMA((2,)),
+            pltpu.SemaphoreType.DMA((2,)),
         ],
         compiler_params=pltpu.CompilerParams(
             collective_id=0, has_side_effects=True, vmem_limit_bytes=63 << 20

time: 194 us -> 191 us (0.985)
  Pallas kernels: 192 us -> 189 us
    pallas_call x1, Pallas kernels: 192 us -> 189 us  [local(): pl.pallas_call(kernel, out_shape=jax.ShapeDtypeStruct((K, PC), F32), in_s...]
where the time goes in v4:
time: 191 us; the launch traced here: 190 us
  Pallas kernels  189 us (99%)
    pallas_call x1, Pallas kernels, local(): pl.pallas_call(kernel, out_shape=jax.ShapeDtypeStruct((K, PC), F32), in_s...  189 us

profile of v4, /device:TPU:1, one launch (start us, length us, event | category | flops | bytes accessed | tf_op | source)
XLA Modules:
  0.0 190.5 jit_solution(14259043127617132131)
XLA Ops:
  0.0 188.9 %shard_map.28 = f32[32,1024]{1,0:T(8,128)} custom-call(bf16[64,16384]{1,0:T(8,128)(2,1)} %stamps.1, f32[32,1024]{1,0:T(8,128)} %bitcast.3), custom_call_target="tpu_custom_call" | custom-call | tf_op jit(solution)/shard_map/pallas_call | solution.py:293
  188.9 1.6 copy.4

commit v5 on v4

--- a/solution.py
+++ b/solution.py
@@ -17,6 +17,7 @@
 PB = PC // 2
 HK = K // 2
 LANES = 128
+BLOCK = 4
 TILES = PB // LANES
 MESH = pl.DeviceIdType.MESH
 NT = (((1,), (1,)), ((), ()))
@@ -39,7 +40,7 @@
 BACK = [OFFSETS.index(((-dx) % GX, (-dy) % GY)) for dx, dy in OFFSETS]
 HOPS = [hops(offset) for offset in OFFSETS]
 FAR_FIRST = sorted(range(1, CHIPS), key=lambda slot: -HOPS[slot])
-GROUPS = [(0, 4), (4, 10), (10, 16)]
+GROUPS = [(0, 4), (4, 12), (12, 16)]
 GROUP_OF = [g for g, (first, last) in enumerate(GROUPS) for _ in range(first, last)]
 Z_STEPS = [2, 1, 3]
 
@@ -55,20 +56,24 @@
     rows = lax.broadcasted_iota(jnp.int32, (K, K), 0)
     cols = lax.broadcasted_iota(jnp.int32, (K, K), 1)
     work = jnp.concatenate([gram, jnp.where(rows == cols, 1.0, 0.0).astype(F32)], axis=1)
-    below = lax.broadcasted_iota(jnp.int32, (K, 1), 0)
-    for j in range(0, K, 2):
-        one, two = work[j : j + 1, :], work[j + 1 : j + 2, :]
-        pivot = lax.rsqrt(one[:, j : j + 1])
-        under = two[:, j : j + 1] * pivot
-        pivot2 = lax.rsqrt(two[:, j + 1 : j + 2] - under * under)
-        row = one * pivot
-        row2 = (two - under * row) * pivot2
-        column = work[:, j : j + 1] * pivot
-        column2 = (work[:, j + 1 : j + 2] - under * column) * pivot2
-        rest = work - column * row - column2 * row2
-        work = jnp.where(
-            below > j + 1, rest, jnp.where(below == j, row, jnp.where(below == j + 1, row2, work))
-        )
+    place = lax.broadcasted_iota(jnp.int32, (K, 2 * K), 0)
+    for j in range(0, K, BLOCK):
+        columns = [jnp.broadcast_to(work[:, j + t : j + t + 1], (K, 2 * K)) for t in range(BLOCK)]
+        rows = [work[j + t : j + t + 1, :] for t in range(BLOCK)]
+        for t in range(BLOCK):
+            pivot = lax.rsqrt(columns[t][j + t : j + t + 1, :])
+            rows[t] = rows[t] * pivot
+            columns[t] = columns[t] * pivot
+            for u in range(t + 1, BLOCK):
+                factor = columns[t][j + u : j + u + 1, :]
+                rows[u] = rows[u] - factor * rows[t]
+                columns[u] = columns[u] - columns[t] * factor
+        rest = work
+        for t in range(BLOCK):
+            rest = rest - columns[t] * rows[t]
+        for t in range(BLOCK):
+            work = jnp.where(place == j + t, rows[t], work)
+        work = jnp.where(place >= j + BLOCK, rest, work)
     return work[:, K:]
 
 
@@ -174,7 +179,7 @@
         place = BACK[slot] * 2 - 1 + c if slot else 0
         send(part1.at[slot, core], got1.at[turn, place], 2, device(slot, core), got_sems.at[turn])
 
-    def add_up_stamps(now, turn, group):
+    def add_up_stamps(now, turn, group, least):
         first, last = GROUPS[group]
         partial = jnp.dot(
             now, blockt[:, first * LANES : last * LANES], preferred_element_type=F32
@@ -185,11 +190,11 @@
                 part1[slot, core, 0] = piece
                 part1[slot ^ 1, core, 1] = piece
         for slot in FAR_FIRST:
-            if first <= slot < last and HOPS[slot] > 1:
+            if first <= slot < last and HOPS[slot] >= least:
                 for core in range(2):
                     send_part(turn, slot, core)
 
-    def spread_stamps(turn):
+    def add_up_nearest(turn):
         for slot in FAR_FIRST:
             if HOPS[slot] == 1:
                 for core in range(2):
@@ -245,30 +250,28 @@
         remote = (last - first) * 2 * ROWS - (ROWS if first == 0 else 0)
         wait_on(block.at[pl.ds(0, remote)], arrival(first))
         blockt[:, first * LANES : last * LANES] = block[first * LANES : last * LANES, :].T
-        add_up_stamps(now, 0, group)
-    spread_stamps(0)
+        add_up_stamps(now, 0, group, 1)
+        if first == 0:
+            send_part(0, 0, other)
     wait(block.at[pl.ds(0, SB - ROWS)], 0)
     gather_stamps(0)
     add_up_pixels(0)
-    panel[...] = sum_pixels(0).astype(BF)
-
-    def sweep(step, carry):
+
+    def sweep(step, now):
         turn = lax.rem(step, 2)
-        now = panel[...]
         for group in range(len(GROUPS)):
-            add_up_stamps(now, turn, group)
-        spread_stamps(turn)
+            add_up_stamps(now, turn, group, 2)
+        add_up_nearest(turn)
         share_gram(turn, gram_of(now))
         gather_stamps(turn)
         share_chip_gram(turn)
         add_up_pixels(turn)
         factor = inverse_cholesky(sum_gram(turn))
-        panel[...] = apply_factor(factor, sum_pixels(turn)).astype(BF)
-        return carry
-
-    lax.fori_loop(1, ITERS, sweep, 0)
-
-    now = panel[...]
+        return apply_factor(factor, sum_pixels(turn)).astype(BF)
+
+    now = lax.fori_loop(1, ITERS, sweep, sum_pixels(0).astype(BF))
+
+    panel[...] = now
     send(panel, pair, 12, device(0, other))
     gram_all[0, c] = pack_gram(gram_of(now))
     for slot in FAR_FIRST:

time: 191 us -> 189 us (0.990)
  Pallas kernels: 189 us -> 187 us
where the time goes in v5:
time: 189 us
  Pallas kernels  187 us (99%)
    pallas_call x1, Pallas kernels, local(): pl.pallas_call(kernel, out_shape=jax.ShapeDtypeStruct((K, PC), F32), in_s...  187 us

profile of v5, /device:TPU:1, one launch (start us, length us, event | category | flops | bytes accessed | tf_op | source)
XLA Modules:
  0.0 188.6 jit_solution(1303748448728176171)
XLA Ops:
  0.0 187.0 %shard_map.28 = f32[32,1024]{1,0:T(8,128)} custom-call(bf16[64,16384]{1,0:T(8,128)(2,1)} %stamps.1, f32[32,1024]{1,0:T(8,128)} %bitcast.3), custom_call_target="tpu_custom_call" | custom-call | tf_op jit(solution)/shard_map/pallas_call | solution.py:296
  187.0 1.6 copy.4

commit v6 on v5

--- a/solution.py
+++ b/solution.py
@@ -40,7 +40,8 @@
 BACK = [OFFSETS.index(((-dx) % GX, (-dy) % GY)) for dx, dy in OFFSETS]
 HOPS = [hops(offset) for offset in OFFSETS]
 FAR_FIRST = sorted(range(1, CHIPS), key=lambda slot: -HOPS[slot])
-GROUPS = [(0, 4), (4, 12), (12, 16)]
+GROUPS = [(0, 2), (2, 6), (6, 10), (10, 14), (14, 16)]
+PUSH = [(0, 2), (2, 10), (10, 14), (14, 16)]
 GROUP_OF = [g for g, (first, last) in enumerate(GROUPS) for _ in range(first, last)]
 Z_STEPS = [2, 1, 3]
 
@@ -180,7 +181,7 @@
         send(part1.at[slot, core], got1.at[turn, place], 2, device(slot, core), got_sems.at[turn])
 
     def add_up_stamps(now, turn, group, least):
-        first, last = GROUPS[group]
+        first, last = group
         partial = jnp.dot(
             now, blockt[:, first * LANES : last * LANES], preferred_element_type=F32
         ).astype(BF)
@@ -218,11 +219,13 @@
         send(both, both, 8, device(0, other), arrival(0))
         wait(got1.at[turn], 2)
 
-    def add_up_pixels(turn):
+    def add_up_pixels(turn, then=None):
         back = jnp.zeros((K, PB), F32)
         for first, last in GROUPS:
             tiles = 2 * (last - first) - (2 if first == 0 else 0)
             wait_on(got1.at[0, pl.ds(0, tiles // 2)], arrival(first))
+            if first == 0 and then is not None:
+                then(turn)
             raw = jnp.concatenate(
                 [jnp.concatenate([proj[i, 0], proj[i, 1]], axis=0) for i in range(first, last)], axis=1
             )
@@ -250,7 +253,7 @@
         remote = (last - first) * 2 * ROWS - (ROWS if first == 0 else 0)
         wait_on(block.at[pl.ds(0, remote)], arrival(first))
         blockt[:, first * LANES : last * LANES] = block[first * LANES : last * LANES, :].T
-        add_up_stamps(now, 0, group, 1)
+        add_up_stamps(now, 0, GROUPS[group], 1)
         if first == 0:
             send_part(0, 0, other)
     wait(block.at[pl.ds(0, SB - ROWS)], 0)
@@ -259,13 +262,12 @@
 
     def sweep(step, now):
         turn = lax.rem(step, 2)
-        for group in range(len(GROUPS)):
+        for group in PUSH:
             add_up_stamps(now, turn, group, 2)
         add_up_nearest(turn)
         share_gram(turn, gram_of(now))
         gather_stamps(turn)
-        share_chip_gram(turn)
-        add_up_pixels(turn)
+        add_up_pixels(turn, share_chip_gram)
         factor = inverse_cholesky(sum_gram(turn))
         return apply_factor(factor, sum_pixels(turn)).astype(BF)
 

time: 189 us -> 186 us (0.984)
  Pallas kernels: 187 us -> 185 us
    pallas_call x1, Pallas kernels: 187 us -> 185 us  [local(): pl.pallas_call(kernel, out_shape=jax.ShapeDtypeStruct((K, PC), F32), in_s...]
where the time goes in v6:
time: 186 us
  Pallas kernels  185 us (99%)
    pallas_call x1, Pallas kernels, local(): pl.pallas_call(kernel, out_shape=jax.ShapeDtypeStruct((K, PC), F32), in_s...  185 us

profile of v6, /device:TPU:1, one launch (start us, length us, event | category | flops | bytes accessed | tf_op | source)
XLA Modules:
  0.0 186.3 jit_solution(12237809054931427717)
XLA Ops:
  0.0 184.7 %shard_map.28 = f32[32,1024]{1,0:T(8,128)} custom-call(bf16[64,16384]{1,0:T(8,128)(2,1)} %stamps.1, f32[32,1024]{1,0:T(8,128)} %bitcast.3), custom_call_target="tpu_custom_call" | custom-call | tf_op jit(solution)/shard_map/pallas_call | solution.py:298
  184.7 1.6 copy.4

commit v7 on v6

--- a/solution.py
+++ b/solution.py
@@ -142,10 +142,12 @@
     def arrival(slot):
         return group_sems.at[GROUP_OF[slot]]
 
-    for slot in sorted(range(1, CHIPS), key=lambda slot: GROUP_OF[slot]):
+    for part in range(2):
+        some = pl.ds(part * (ROWS // 2), ROWS // 2)
         for core in range(2):
-            to = device(slot, core)
-            send(pixels_of(to, core), rows_of(BACK[slot]), 0, to, arrival(BACK[slot]))
+            for slot in range(1, CHIPS):
+                to = device(slot, core)
+                send(pixels_of(to, core).at[some], rows_of(BACK[slot]).at[some], 0, to, arrival(BACK[slot]))
     to = device(0, other)
     send(pixels_of(to, other), rows_of(0), 0, to, arrival(0))
     own = pltpu.make_async_copy(pixels_of(device(0, c), c), rows_of(0), sems.at[14])
@@ -239,7 +241,6 @@
 
     def sum_pixels(turn):
         wait_on(sums.at[turn, pl.ds(0, GZ - 1)], z_sems.at[turn])
-        wait(sums.at[turn, pl.ds(0, GZ - 1)], 10)
         total = sums[turn, 0].astype(F32)
         for i in range(1, GZ):
             total = total + sums[turn, i].astype(F32)
@@ -265,6 +266,7 @@
         for group in PUSH:
             add_up_stamps(now, turn, group, 2)
         add_up_nearest(turn)
+        wait(sums.at[0, pl.ds(0, GZ - 1)], 10)
         share_gram(turn, gram_of(now))
         gather_stamps(turn)
         add_up_pixels(turn, share_chip_gram)
@@ -273,6 +275,7 @@
 
     now = lax.fori_loop(1, ITERS, sweep, sum_pixels(0).astype(BF))
 
+    wait(sums.at[0, pl.ds(0, GZ - 1)], 10)
     panel[...] = now
     send(panel, pair, 12, device(0, other))
     gram_all[0, c] = pack_gram(gram_of(now))

time: 186 us -> 186 us (level)
  no operation moved by 1% of the time
where the time goes in v7:
time: 186 us
  Pallas kernels  184 us (99%)
    pallas_call x1, Pallas kernels, local(): pl.pallas_call(kernel, out_shape=jax.ShapeDtypeStruct((K, PC), F32), in_s...  184 us

profile of v7, /device:TPU:1, one launch (start us, length us, event | category | flops | bytes accessed | tf_op | source)
XLA Modules:
  0.0 185.6 jit_solution(2828336340571941492)
XLA Ops:
  0.0 184.0 %shard_map.28 = f32[32,1024]{1,0:T(8,128)} custom-call(bf16[64,16384]{1,0:T(8,128)(2,1)} %stamps.1, f32[32,1024]{1,0:T(8,128)} %bitcast.3), custom_call_target="tpu_custom_call" | custom-call | tf_op jit(solution)/shard_map/pallas_call | solution.py:301
  184.0 1.6 copy.4
